TPU v7x, 128 devices: a whole 4x4x4 slice. The times are simulated.
128 devices in a mesh: chain: 2 (over core), energy: 64 (over z, y, x).
Axes of the slice: x: 4, y: 4, z: 4, core: 2. Of those that a mesh axis runs over, the one named last changes fastest.
Arguments:
- retarded: float32 [64, 4, 2, 256, 256], P('energy', 'chain'), may hold values from -0.625 to 0.625
- lesser_sigma: float32 [64, 4, 2, 256, 256], P('energy', 'chain'), may hold values from -6 to 6
- coupling: float32 [4, 2, 256, 256], P('chain'), may hold values from -1 to 1
- coupling_pattern: int32 [4, 4, 4], P('chain'), may hold values from 0 to 1, as said below
- kept_blocks: int32 [4], replicated, may hold values from 0 to 15, as said below
- lead_lesser: float32 [64, 2, 256, 256], P('energy'), may hold values from -8 to 8
Outputs:
- polarization: float32 [16, 2, 65536], P(None, None, ('chain', 'energy'))
Inputs may be any that keep to these rules, and one draw needn't show every extreme that they name: `coupling_pattern`: 0/1 entries; each cell's coupling has exactly 4 ones. `kept_blocks`: distinct block numbers.
All inputs are finite; a program needn't handle non-finite values.
Results may differ from a plain program's by a relative error of at most 0.0001.
Values sent between devices are 32-bit elements; how exact they have to be, the bound alone decides.
A program may use at most 832 MiB of HBM per device.

v0:
```python
import jax
import jax.numpy as jnp
from jax import lax
from jax.sharding import Mesh
from jax.sharding import PartitionSpec as P

M = 256
BLOCK = 64
NBLK = 4
KEEP = 4
LAGS = 16
ENERGY = ("energy_0", "energy_1", "energy_2")
CHAIN_ENERGY = ("chain", "energy_0", "energy_1", "energy_2")


def passed_along(value, axis, steps):
    count = lax.axis_size(axis)
    leading, last = (max(0, -steps), min(count, count - steps))
    return lax.ppermute(value, axis, [(source, source + steps) for source in range(leading, last)])


def in_blocks(shard, dim, peers):
    lengths = shard.shape
    tiles = shard.reshape(*lengths[:dim], peers, lengths[dim] // peers, *lengths[dim + 1 :])
    return jnp.moveaxis(tiles, dim, 0)


def laid_out(tiles, dim):
    tiles = jnp.moveaxis(tiles, 0, dim)
    lengths = tiles.shape
    return tiles.reshape(*lengths[:dim], lengths[dim] * lengths[dim + 1], *lengths[dim + 2 :])


def exchange_in_order(tiles, axes, turns):
    inside = tiles.shape[1:]
    result = tiles.reshape(*(lax.axis_size(a) for a in axes), *inside)
    for k in turns:
        result = lax.all_to_all(result, axes[k], k, k, tiled=True)
    return result.reshape(-1, *inside)


def one_axis_at_a_time(shard, axes, turns, split_dim, concat_dim):
    tiles = in_blocks(shard, split_dim, lax.axis_size(axes))
    return laid_out(exchange_in_order(tiles, axes, turns), concat_dim)


def times_plain(left, right):
    return jnp.einsum("...ij,...jk->...ik", left, right, precision=lax.Precision.HIGHEST)


def times_transposed(left, right):
    return jnp.einsum("...ij,...kj->...ik", left, right, precision=lax.Precision.HIGHEST)


def complex_product(left, right):
    left_re, left_im = (left[..., 0, :, :], left[..., 1, :, :])
    right_re, right_im = (right[..., 0, :, :], right[..., 1, :, :])
    first = times_plain(left_re, right_re)
    second = times_plain(left_im, right_im)
    mixed = times_plain(left_re + left_im, right_re + right_im)
    return jnp.stack([first - second, mixed - first - second], axis=-3)


def product_adjoint(left, right):
    left_re, left_im = (left[..., 0, :, :], left[..., 1, :, :])
    right_re, right_im = (right[..., 0, :, :], right[..., 1, :, :])
    first = times_transposed(left_re, right_re)
    second = times_transposed(left_im, right_im)
    mixed = times_transposed(left_re + left_im, right_re - right_im)
    return jnp.stack([first + second, mixed - first + second], axis=-3)


def expand_pattern(pattern):
    return jnp.repeat(jnp.repeat(pattern.astype(jnp.float32), BLOCK, axis=-2), BLOCK, axis=-1)


def pick_blocks(matrix, kept_blocks):
    lead_shape = matrix.shape[:-2]
    tiles = matrix.reshape(lead_shape + (NBLK, BLOCK, NBLK, BLOCK))
    tiles = jnp.swapaxes(tiles, -3, -2)
    tiles = tiles.reshape(lead_shape + (NBLK * NBLK, BLOCK * BLOCK))
    return jnp.take(tiles, kept_blocks, axis=-2)


def per_device(retarded, lesser_sigma, coupling, coupling_pattern, kept_blocks, lead_lesser):
    energies_here = retarded.shape[0]
    cell_count = retarded.shape[1]
    span_width = cell_count * KEEP * BLOCK * BLOCK
    coupling_full = coupling * expand_pattern(coupling_pattern)[:, None]
    joined_all = complex_product(retarded, coupling_full[None])
    fresh_all = product_adjoint(complex_product(retarded, lesser_sigma), retarded)
    position = lax.axis_index("chain")
    length = lax.axis_size("chain")

    def advance(state_in, per_group):
        pieces = []
        for cell_index in range(cell_count):
            bridge = joined_all[:, cell_index]
            state_in = fresh_all[:, cell_index] + product_adjoint(
                complex_product(bridge, state_in), bridge
            )
            pieces.append(pick_blocks(state_in, kept_blocks))
        stacked = jnp.stack(pieces, axis=2)
        return (state_in, stacked.reshape(per_group, 2, span_width))

    def send_whole(leaving):
        return passed_along(leaving, "chain", 1)

    per_group = energies_here // 1
    tick_total = 1 + length - 1
    buffer = jnp.zeros((energies_here, 2, span_width), jnp.float32)

    def tick(tick_index, state):
        incoming, buffer = state
        micro_batch = tick_index - position
        active = jnp.logical_and(micro_batch >= 0, micro_batch < 1)
        batch_slot = jnp.clip(micro_batch, 0, 1 - 1)
        offset = batch_slot * per_group
        entering = jnp.where(position == 0, lead_lesser, incoming)

        def working(operands):
            entering_now, buffer_now = operands
            leaving, retained = advance(entering_now, per_group)
            return (leaving, lax.dynamic_update_slice_in_dim(buffer_now, retained, offset, 0))

        def waiting(operands):
            entering_now, buffer_now = operands
            return (jnp.zeros_like(entering_now), buffer_now)

        leaving, buffer = lax.cond(active, working, waiting, (entering, buffer))
        return (send_whole(leaving), buffer)

    initial = (jnp.zeros((per_group, 2, M, M), jnp.float32), buffer)
    _, buffer = lax.fori_loop(0, tick_total, tick, initial)
    retained = buffer
    owners = one_axis_at_a_time(retained, ENERGY, (0, 1, 2), 2, 0)
    energy_total = owners.shape[0]
    results = []
    for lag_index in range(LAGS):
        shifted = owners[lag_index:]
        earlier = owners[: energy_total - lag_index]
        real_part = jnp.sum(shifted[:, 0] * earlier[:, 0] + shifted[:, 1] * earlier[:, 1], axis=0)
        imag_part = jnp.sum(shifted[:, 1] * earlier[:, 0] - shifted[:, 0] * earlier[:, 1], axis=0)
        results.append(jnp.stack([real_part, imag_part], axis=0))
    return jnp.stack(results, axis=0) / jnp.float32(energy_total)


def solution(mesh):
    finer = Mesh(
        mesh.devices.reshape(mesh.shape["chain"], 4, 4, 4),
        ("chain", "energy_0", "energy_1", "energy_2"),
    )
    placed = (
        P(ENERGY, "chain", None, None, None),
        P(ENERGY, "chain", None, None, None),
        P("chain", None, None, None),
        P("chain", None, None),
        P(),
        P(ENERGY, None, None, None),
    )
    return jax.shard_map(
        per_device,
        mesh=finer,
        in_specs=placed,
        out_specs=P(None, None, CHAIN_ENERGY),
        check_vma=False,
    )
```

profile of v0, /device:TPU:0, one launch (start us, length us, event | category | flops | bytes accessed | tf_op | source)
XLA Modules:
  0.0 111.1 jit_solution(12003443806861216591)
XLA Ops:
  0.0 1.9 %fusion.71 = f32[2,256,256]{2,1,0:T(8,128)S(1)} fusion(f32[1,2,2,256,256]{4,3,2,1,0:T(8,128)} %param.13, f32[1,2,2,256,256]{4,3,2,1,0:T(8,128)} %param.12), kind=kOutput, calls=%fused_computation.107 | convolution fusion | flops 402653184 | bytes 1572864 | tf_op jit(solution)/shard_map/...ij,...jk->...ik/dot_general | solution.py:48
  2.0 1.8 %fusion.78 = f32[2,256,256]{2,1,0:T(8,128)S(1)} fusion(f32[1,2,2,256,256]{4,3,2,1,0:T(8,128)} %param.13, f32[1,2,2,256,256]{4,3,2,1,0:T(8,128)S(1)} %copy-done.7), kind=kOutput, calls=%fused_computation.116 | convolution fusion | flops 402653184 | bytes 1572864 | tf_op jit(solution)/shard_map/...ij,...jk->...ik/dot_general | solution.py:48
  3.8 0.7 fusion.70
  4.5 0.7 fusion.82
  5.9 0.8 fusion.69
  6.7 1.6 %copy.76 = f32[2,2,256,256]{2,3,0,1:T(8,128)S(1)} copy(f32[2,2,256,256]{3,2,1,0:T(8,128)} %param.14) | data formatting | bytes 2097152 | tf_op args[2]
  10.1 0.7 fusion.67
  11.1 1.3 %copy.80 = f32[1,2,2,256,256]{4,3,2,1,0:T(8,128)} copy(f32[1,2,2,256,256]{3,4,1,2,0:T(8,128)S(1)} %pad_maximum_fusion.2) | data formatting | bytes 2097152 | tf_op jit(solution)/shard_map/while | solution.py:134
  13.1 56.2 %while.19 = (s32[]{:T(128)}, f32[1,2,256,256]{3,2,1,0:T(8,128)S(1)}, f32[1,2,32768]{2,1,0:T(2,128)S(1)}, s32[]{:T(128)}, f32[1,2,2,256,256]{4,3,2,1,0:T(8,128)S(...) while((s32[]{:T(128)}, ...), condition=%wide.region_3.0_spmd, body=%wide.region_0.4_spmd.sunk | while | flops 2418672640 | bytes 50336296 | solution.py:134
  13.1 25.1 %conditional.2 = (f32[1,2,256,256]{3,2,1,0:T(8,128)}, f32[1,2,32768]{2,1,0:T(2,128)S(1)}) conditional(s32[]{:T(128)} %convert_element_type.13, f32[1,2,32768]{2,1,0:T(2,128)S(1)} %get-tuple-element.391, (f32[1,2,2,256,256]{4,3,2,1,0:T(8,128)S(1)}, pred[]{:T(512)}, f32[1,2,256,256]{3,2,1,0:T(8,128)}, f32[1,2,256,256]{3,2,1,0:T(8,128)S(1)}, ...), branch_computations={%region_1.1_spmd, %region_2.3_spmd} | conditional | flops 2418672640 | bytes 48238908 | solution.py:130
  13.1 1.3 %slice_bitcast_fusion = (f32[1,2,256,256]{3,2,1,0:T(8,128)S(1)}, f32[1,2,256,256]{3,2,1,0:T(8,128)S(1)}) fusion(f32[1,2,2,256,256]{4,3,2,1,0:T(8,128)} %get-tuple-element.203), kind=kLoop, calls=%fused_computation.22 | loop fusion | bytes 2097152 | tf_op jit(solution)/shard_map/while/body/eval_jaxpr/cond/branch_1_fun/squeeze | solution.py:98
  14.4 1.1 %broadcast_select_fusion = f32[1,2,256,256]{3,2,1,0:T(8,128)S(1)} fusion(f32[1,2,256,256]{3,2,1,0:T(8,128)} %get-tuple-element.201, f32[1,2,256,256]{3,2,1,0:T(8,128)S(1)} %get-tuple-element.202, pred[]{:T(512)} %get-tuple-element.200), kind=kLoop, calls=%fused_computation.55 | loop fusion | flops 131072 | bytes 1572865 | tf_op jit(solution)/shard_map/while/body/eval_jaxpr/jit(_where)/select_n | solution.py:119
  23.9 0.9 copy.68
  25.0 0.9 copy.67
  25.8 0.9 fusion.101
  27.2 1.4 %fusion.5 = f32[1,2,4,4,64,64]{5,4,3,2,1,0:T(8,128)S(1)} fusion(f32[1,1,4,64,4,64]{5,3,4,2,1,0:T(8,128)} %copy.68, f32[1,1,4,64,4,64]{5,3,4,2,1,0:T(8,128)} %copy.67, f32[1,2,4,64,4,64]{5,4,3,2,1,0:T(4,128)S(1)} %squeeze.13), kind=kLoop, calls=%fused_computation.17 | loop fusion | flops 262144 | bytes 1572864 | tf_op jit(solution)/shard_map/while/body/eval_jaxpr/cond/branch_1_fun/transpose | solution.py:80
  29.4 0.7 gather_fusion.1
  30.5 0.9 copy.64
  31.7 0.9 copy.63
  33.4 1.4 %fusion.4 = f32[1,2,4,4,64,64]{5,4,3,2,1,0:T(8,128)S(1)} fusion(f32[1,1,4,64,4,64]{5,3,4,2,1,0:T(8,128)} %copy.64, f32[1,1,4,64,4,64]{5,3,4,2,1,0:T(8,128)} %copy.63, f32[1,2,4,64,4,64]{5,4,3,2,1,0:T(4,128)S(1)} %squeeze.12), kind=kLoop, calls=%fused_computation.15 | loop fusion | flops 262144 | bytes 1572864 | tf_op jit(solution)/shard_map/while/body/eval_jaxpr/cond/branch_1_fun/transpose | solution.py:80
  35.5 0.7 gather_fusion
  36.6 0.8 copy-done.3
  37.4 0.9 maximum_add_fusion.3
  38.3 1.3 %collective-permute-start = (f32[1,2,256,256]{3,2,1,0:T(8,128)}, f32[1,2,256,256]{3,2,1,0:T(8,128)S(1)}, u32[]{:S(2)}, u32[]{:S(2)}) collective-permute-start(f32[1,2,256,256]{3,2,1,0:T(8,128)} %get-tuple-element.372), channel_id=1, source_target_pairs={{0,64},{1,65},{2,66},{3,67},{4,68},{5,69},{6,70},{7,71},{8,72},{9,... | collective-permute-start | bytes 1572872 | tf_op jit(solution)/shard_map/while/body/eval_jaxpr/ppermute | solution.py:19
  39.6 1.7 %collective-permute-done = f32[1,2,256,256]{3,2,1,0:T(8,128)S(1)} collective-permute-done((f32[1,2,256,256]{3,2,1,0:T(8,128)}, f32[1,2,256,256]{3,2,1,0:T(8,128)S(1)}, u32[]{:S(2)}, u32[]{:S(2)}) %collective-permute-start) | collective-permute-done | bytes 524320 | tf_op jit(solution)/shard_map/while/body/eval_jaxpr/ppermute | solution.py:19
  41.3 0.9 conditional.2
  41.3 0.9 broadcast.31
  42.1 25.5 %collective-permute-start = (f32[1,2,256,256]{3,2,1,0:T(8,128)}, f32[1,2,256,256]{3,2,1,0:T(8,128)S(1)}, u32[]{:S(2)}, u32[]{:S(2)}) collective-permute-start(f32[1,2,256,256]{3,2,1,0:T(8,128)} %get-tuple-element.372), channel_id=1, source_target_pairs={{0,64},{1,65},{2,66},{3,67},{4,68},{5,69},{6,70},{7,71},{8,72},{9,... | collective-permute-start | bytes 1572872 | tf_op jit(solution)/shard_map/while/body/eval_jaxpr/ppermute | solution.py:19
  67.7 1.7 %collective-permute-done = f32[1,2,256,256]{3,2,1,0:T(8,128)S(1)} collective-permute-done((f32[1,2,256,256]{3,2,1,0:T(8,128)}, f32[1,2,256,256]{3,2,1,0:T(8,128)S(1)}, u32[]{:S(2)}, u32[]{:S(2)}) %collective-permute-start) | collective-permute-done | bytes 524320 | tf_op jit(solution)/shard_map/while/body/eval_jaxpr/ppermute | solution.py:19
  69.4 12.4 %all_to_all.15 = f32[4,4,4,1,2,512]{5,2,1,4,3,0:T(4,128)S(1)} all-to-all(f32[4,4,4,1,2,512]{5,2,1,4,3,0:T(4,128)S(1)} %copy.82), channel_id=1, replica_groups=mesh['chain'=2,'energy_0'=4,'energy_1'=4,'energy_2'=4] {'energy_0'}, dimensions={0} | all-to-all | bytes 524288 | tf_op jit(solution)/shard_map/all_to_all | solution.py:38
  81.9 10.9 %all_to_all.16 = f32[4,4,4,1,2,512]{5,2,0,4,3,1:T(4,128)S(1)} all-to-all(f32[4,4,4,1,2,512]{5,2,0,4,3,1:T(4,128)S(1)} %copy.83), channel_id=1, replica_groups=mesh['chain'=2,'energy_0'=4,'energy_1'=4,'energy_2'=4] {'energy_1'}, dimensions={1} | all-to-all | bytes 524288 | tf_op jit(solution)/shard_map/all_to_all | solution.py:38
  93.0 10.8 %all_to_all.17 = f32[4,4,4,1,2,512]{5,1,0,4,3,2:T(4,128)S(1)} all-to-all(f32[4,4,4,1,2,512]{5,1,0,4,3,2:T(4,128)S(1)} %copy.84), channel_id=1, replica_groups=mesh['chain'=2,'energy_0'=4,'energy_1'=4,'energy_2'=4] {'energy_2'}, dimensions={2} | all-to-all | bytes 524288 | tf_op jit(solution)/shard_map/all_to_all | solution.py:38
  (102 shorter events, 23.2 us)
Async XLA Ops:
  0.0 2.0 %copy-start.7 = (f32[1,2,2,256,256]{4,3,2,1,0:T(8,128)S(1)}, f32[1,2,2,256,256]{4,3,2,1,0:T(8,128)}, u32[]{:S(2)}) copy-start(f32[1,2,2,256,256]{4,3,2,1,0:T(8,128)} %param.12) | copy-start | bytes 3145732
  2.0 1.8 %copy-start.8 = (f32[1,2,2,256,256]{4,3,2,1,0:T(8,128)S(1)}, f32[1,2,2,256,256]{4,3,2,1,0:T(8,128)}, u32[]{:S(2)}) copy-start(f32[1,2,2,256,256]{4,3,2,1,0:T(8,128)} %param.13) | copy-start | bytes 3145732
  6.7 1.6 %copy-start.9 = (s32[2,4,4]{2,1,0:T(4,128)S(1)}, s32[2,4,4]{2,1,0:T(4,128)}, u32[]{:S(2)}) copy-start(s32[2,4,4]{2,1,0:T(4,128)} %param.15) | copy-start | bytes 388
  12.5 0.7 copy-start.10
  18.6 0.7 copy-start.4
  19.2 0.7 copy-start
  23.0 1.8 %copy-start.2 = (f32[256,256]{1,0:T(8,128)}, f32[256,256]{1,0:T(8,128)S(1)}, u32[]{:S(2)}) copy-start(f32[256,256]{1,0:T(8,128)S(1)} %get-tuple-element.313) | copy-start | bytes 786436 | tf_op jit(solution)/shard_map/while/body/eval_jaxpr/cond
  29.3 1.0 copy-start.1
  30.5 1.0 copy-start.5
  31.7 1.2 %copy-start.6 = (f32[1,1,2,256,256]{4,3,2,1,0:T(8,128)S(1)}, f32[1,1,2,256,256]{4,3,2,1,0:T(8,128)}, u32[]{:S(2)}) copy-start(f32[1,1,2,256,256]{4,3,2,1,0:T(8,128)} %get-tuple-element.305) | copy-start | bytes 1572868 | tf_op jit(solution)/shard_map/while/body/eval_jaxpr/cond
  36.4 1.0 copy-start.3
  38.3 3.0 %collective-permute-start = (f32[1,2,256,256]{3,2,1,0:T(8,128)}, f32[1,2,256,256]{3,2,1,0:T(8,128)S(1)}, u32[]{:S(2)}, u32[]{:S(2)}) collective-permute-start(f32[1,2,256,256]{3,2,1,0:T(8,128)} %get-tuple-element.372), channel_id=1, source_target_pairs={{0,64},{1,65},{2,66},{3,67},{4,68},{5,69},{6,70},{7,71},{8,72},{9,... | collective-permute-start | bytes 1572872 | tf_op jit(solution)/shard_map/while/body/eval_jaxpr/ppermute | solution.py:19
  42.1 27.2 %collective-permute-start = (f32[1,2,256,256]{3,2,1,0:T(8,128)}, f32[1,2,256,256]{3,2,1,0:T(8,128)S(1)}, u32[]{:S(2)}, u32[]{:S(2)}) collective-permute-start(f32[1,2,256,256]{3,2,1,0:T(8,128)} %get-tuple-element.372), channel_id=1, source_target_pairs={{0,64},{1,65},{2,66},{3,67},{4,68},{5,69},{6,70},{7,71},{8,72},{9,... | collective-permute-start | bytes 1572872 | tf_op jit(solution)/shard_map/while/body/eval_jaxpr/ppermute | solution.py:19
where the time goes:
time: 112 us; the launch traced here: 111 us
  blocking collectives  34.1 us (30%)
  starting transfers between devices  26.8 us (24%)
  local copies, waits for them, and re-layouts  17.8 us (16%)
  matrix products  15.8 us (14%)
  other arithmetic  12.5 us (11%)
  waiting for transfers between devices  3.39 us (3%)
    all_to_all x3, blocking collectives, exchange_in_order(): result = lax.all_to_all(result, axes[k], k, k, tiled=True)  34.1 us
    ppermute x2, starting transfers between devices, passed_along(): lax.ppermute(value, axis, [(source, source + steps) for source in range(l...  26.8 us
    dot_general x12, matrix products, times_plain(): jnp.einsum('...ij,...jk->...ik', left, right, precision=lax.Precision.HIG...  10 us
    reduce_sum x16, other arithmetic, per_device(): jnp.sum(shifted[:, 0] * earlier[:, 0] + shifted[:, 1] * earlier[:, 1], ax...  6.09 us
    dot_general x9, matrix products, times_transposed(): jnp.einsum('...ij,...kj->...ik', left, right, precision=lax.Precision.HIG...  5.74 us
    another operation x8, local copies, waits for them, and re-layouts, product_adjoint(): return jnp.stack([first + second, mixed - first + second], axis=-3)  4.41 us
    ppermute x2, waiting for transfers between devices, passed_along(): lax.ppermute(value, axis, [(source, source + steps) for source in range(l...  3.39 us
    transpose x2, other arithmetic, pick_blocks(): tiles = jnp.swapaxes(tiles, -3, -2)  2.71 us
  transfers between devices with their start and end apart: 2, of which 2 were waited for; matrix products, arithmetic and copies ran while one was open for 0% of the time, Pallas kernels for 0%

commit v1 on v0

v1 whole, which is shorter than its diff:
```python
import functools

import jax
import jax.numpy as jnp
from jax import lax
from jax.experimental import pallas as pl
from jax.experimental.pallas import tpu as pltpu
from jax.sharding import PartitionSpec as P

M = 256
BLOCK = 64
NBLK = 4
KEEP = 4
LAGS = 16
ENERGIES = 64
SIDE = 4
MESH = pl.DeviceIdType.MESH
ADJ = (((1,), (1,)), ((), ()))
PLAIN = (((1,), (0,)), ((), ()))


def split(x):
    high = x.astype(jnp.bfloat16)
    return high, (x - high.astype(jnp.float32)).astype(jnp.bfloat16)


def dot3(left_h, left_l, right, dims):
    right_h, right_l = split(right)
    return lax.dot_general(
        jnp.concatenate([left_h, left_h, left_l], 1),
        jnp.concatenate([right_h, right_l, right_h], 1 if dims is ADJ else 0),
        dims,
        preferred_element_type=jnp.float32,
    )


class Left:
    def __init__(self, high, low):
        self.high, self.low = high, low

    def fill(self, re, im):
        for i, part in enumerate((re, im, re + im)):
            self.high[i], self.low[i] = split(part)

    def three(self, a, b, c, dims):
        return [dot3(self.high[i], self.low[i], x, dims) for i, x in enumerate((a, b, c))]

    def adjoint(self, re, im):
        p, q, s = self.three(re, im, re - im, ADJ)
        return p + q, s - p + q

    def plain(self, re, im):
        p, q, s = self.three(re, im, re + im, PLAIN)
        return p - q, s - p - q


def choose(which, blocks):
    out = blocks[-1]
    for i in range(len(blocks) - 2, -1, -1):
        out = jnp.where(which == i, blocks[i], out)
    return out


def row_blocks(part):
    return [part[i * BLOCK : (i + 1) * BLOCK] for i in range(NBLK)]


def kept_left(rows_ref, re, im, kept_rows):
    for k in range(KEEP):
        for i, part in enumerate((re, im)):
            high, low = split(choose(kept_rows[k], row_blocks(part)))
            rows_ref[k, :BLOCK, i * M : (i + 1) * M] = high
            rows_ref[k, BLOCK:, i * M : (i + 1) * M] = low


def kept_tiles(rows_ref, re, im, kept_cols):
    out = []
    for k in range(KEEP):
        re_h, re_l = split(choose(kept_cols[k], row_blocks(re)))
        im_h, im_l = split(choose(kept_cols[k], row_blocks(im)))
        stack = []
        for x, y in ((re_h, im_h), (re_l, im_l)):
            stack += [jnp.concatenate([x, y], 1), jnp.concatenate([-y, x], 1)]
        o = lax.dot_general(rows_ref[k], jnp.concatenate(stack, 0), ADJ, preferred_element_type=jnp.float32)
        o = o[:BLOCK] + o[BLOCK:]
        out.append(o[:, :128] + o[:, 128:])
    return out


def kernel(
    pattern_ref, kept_ref, g_hbm, s_hbm, b_hbm, lead_hbm, out_ref,
    g_in, s_in, b_in, lead_in, left_h, left_l, rows, right, passed, entered, send, recv, sums,
    in_sem, pass_sem, send_sem, recv_sem,
):
    chain, me = lax.axis_index("chain"), lax.axis_index("energy")
    my_y, my_x = lax.rem(lax.div(me, SIDE), SIDE), lax.rem(me, SIDE)

    def load(i, source, target):
        return pltpu.make_async_copy(source, target, in_sem.at[i])

    loads = {}
    for cell in range(2):
        loads["b", cell] = load(cell, b_hbm.at[cell], b_in.at[cell])
        loads["s", cell] = load(2 + cell, s_hbm.at[0, cell], s_in.at[cell])
        loads["g", cell] = load(4 + cell, g_hbm.at[0, cell], g_in.at[cell])
    loads["lead"] = load(6, lead_hbm.at[0], lead_in)
    for name in (("b", 0), "lead", ("s", 0), ("g", 0), ("b", 1), ("s", 1), ("g", 1)):
        loads[name].start()

    barrier = pltpu.get_barrier_semaphore()

    @pl.loop(1, ENERGIES)
    def _(step):
        pl.semaphore_signal(
            barrier, inc=1, device_id={"energy": lax.rem(me + step, ENERGIES)}, device_id_type=MESH
        )

    pl.semaphore_signal(barrier, inc=1, device_id={"chain": 1 - chain}, device_id_type=MESH)

    recv[pl.ds(ENERGIES, LAGS)] = jnp.zeros((LAGS, 8, 128), jnp.float32)
    lefts = [Left(left_h.at[i], left_l.at[i]) for i in range(5)]
    lane = lax.broadcasted_iota(jnp.int32, (BLOCK, 128), 1) < BLOCK

    def masked_coupling(cell):
        parts = []
        for part in range(2):
            rows = []
            for r in range(NBLK):
                strip = b_in[cell, part, r * BLOCK : (r + 1) * BLOCK, :]
                halves = []
                for t in range(NBLK // 2):
                    pair = [pattern_ref[cell, r, 2 * t + h].astype(jnp.float32) for h in range(2)]
                    halves.append(strip[:, t * 128 : (t + 1) * 128] * jnp.where(lane, pair[0], pair[1]))
                rows.append(jnp.concatenate(halves, 1))
            parts.append(jnp.concatenate(rows, 0))
        return parts

    numbers = [jnp.full((BLOCK, M), kept_ref[k], jnp.int32) for k in range(KEEP)]
    kept_rows = [jnp.right_shift(n, 2) for n in numbers]
    kept_cols = [jnp.bitwise_and(n, 3) for n in numbers]

    def keep_right(slot, re, im):
        right[slot, 0], right[slot, 1] = re, im

    def tiles_of(slot):
        return kept_tiles(rows.at[slot], right[slot, 0], right[slot, 1], kept_cols)

    def put(cell, tiles):
        for k, tile in enumerate(tiles):
            for row in range(8):
                send[cell * 32 + k * 8 + row] = tile[row * 8 : row * 8 + 8]

    def spread(cell):
        @pl.loop(0, 32)
        def _(step):
            z = 2 * cell + lax.div(step, 16)
            y = lax.rem(my_y + 2 + lax.rem(lax.div(step, 4), 4), SIDE)
            x = lax.rem(my_x + 2 + lax.rem(step, 4), SIDE)
            owner = (z * SIDE + y) * SIDE + x

            @pl.when(owner == me)
            def _():
                pltpu.make_async_copy(send.at[owner], recv.at[me], recv_sem).start()

            @pl.when(owner != me)
            def _():
                pltpu.make_async_remote_copy(
                    src_ref=send.at[owner], dst_ref=recv.at[me], send_sem=send_sem, recv_sem=recv_sem,
                    device_id={"energy": owner}, device_id_type=MESH,
                ).start()

    passing = pltpu.make_async_remote_copy(
        src_ref=passed, dst_ref=entered, send_sem=pass_sem.at[0], recv_sem=pass_sem.at[1],
        device_id={"chain": 1}, device_id_type=MESH,
    )

    @pl.when(chain == 0)
    def _():
        loads["b", 0].wait()
        b0, g0, b1, g1 = lefts[:4]
        b0.fill(*masked_coupling(0))
        loads["lead"].wait()
        re, im = b0.adjoint(*b0.adjoint(lead_in[0], lead_in[1]))
        loads["s", 0].wait()
        x_re, x_im = s_in[0, 0] + re, s_in[0, 1] + im
        loads["g", 0].wait()
        g0.fill(g_in[0, 0], g_in[0, 1])
        y_re, y_im = g0.adjoint(x_re, x_im)
        keep_right(0, y_re, y_im)
        state = g0.adjoint(y_re, y_im)
        loads["b", 1].wait()
        b1.fill(*masked_coupling(1))
        re, im = b1.adjoint(*b1.adjoint(*state))
        loads["s", 1].wait()
        x_re, x_im = s_in[1, 0] + re, s_in[1, 1] + im
        loads["g", 1].wait()
        g1.fill(g_in[1, 0], g_in[1, 1])
        y_re, y_im = g1.adjoint(x_re, x_im)
        keep_right(1, y_re, y_im)
        passed[0], passed[1] = g1.adjoint(y_re, y_im)
        pl.semaphore_wait(barrier, ENERGIES)
        passing.start()
        kept_left(rows.at[0], g_in[0, 0], g_in[0, 1], kept_rows)
        put(0, tiles_of(0))
        spread(0)
        kept_left(rows.at[1], g_in[1, 0], g_in[1, 1], kept_rows)
        put(1, tiles_of(1))
        spread(1)
        passing.wait_send()

    @pl.when(chain == 1)
    def _():
        g2, b3, g3, a2, c3 = lefts
        loads["s", 0].wait()
        loads["g", 0].wait()
        g2.fill(g_in[0, 0], g_in[0, 1])
        y_re, y_im = g2.adjoint(s_in[0, 0], s_in[0, 1])
        keep_right(0, y_re, y_im)
        fresh = g2.adjoint(y_re, y_im)
        kept_left(rows.at[0], g_in[0, 0], g_in[0, 1], kept_rows)
        put(0, tiles_of(0))
        loads["b", 0].wait()
        joined = g2.plain(*masked_coupling(0))
        a2.fill(*joined)
        loads["b", 1].wait()
        b3.fill(*masked_coupling(1))
        re, im = b3.adjoint(*b3.adjoint(*fresh))
        loads["s", 1].wait()
        x_re, x_im = s_in[1, 0] + re, s_in[1, 1] + im
        loads["g", 1].wait()
        g3.fill(g_in[1, 0], g_in[1, 1])
        y_re, y_im = g3.adjoint(x_re, x_im)
        keep_right(1, y_re, y_im)
        kept_left(rows.at[1], g_in[1, 0], g_in[1, 1], kept_rows)
        put(1, tiles_of(1))
        c3_re, c3_im = g3.plain(*b3.plain(*joined))
        c3.fill(c3_re, c3_im)
        kept_left(rows.at[2], *joined, kept_rows)
        kept_left(rows.at[3], c3_re, c3_im, kept_rows)
        loads["lead"].wait()
        pl.semaphore_wait(barrier, ENERGIES)
        passing.wait_recv()
        for cell, left in ((0, a2), (1, c3)):
            keep_right(cell, *left.adjoint(entered[0], entered[1]))
            tiles = kept_tiles(rows.at[2 + cell], right[cell, 0], right[cell, 1], kept_cols)
            for k in range(KEEP):
                for row in range(8):
                    at = cell * 32 + k * 8 + row
                    send[at] = send[at] + tiles[k][row * 8 : row * 8 + 8]
            spread(cell)

    everyone = recv.at[pl.ds(0, ENERGIES)]
    pltpu.make_async_copy(everyone, everyone, recv_sem).wait()

    def lag_step(step, carry):
        first, second = list(carry[:LAGS]), list(carry[LAGS:])
        window = [recv[step * 4 + i] for i in range(LAGS + 3)]
        for i in range(4):
            earlier = window[i]
            swapped = pltpu.roll(earlier, BLOCK, 1)
            for lag in range(LAGS):
                first[lag] += window[i + lag] * earlier
                second[lag] += window[i + lag] * swapped
        return (*first, *second)

    totals = lax.fori_loop(0, ENERGIES // 4, lag_step, (jnp.zeros((8, 128), jnp.float32),) * (2 * LAGS))
    for lag in range(LAGS):
        p, q = totals[lag] * (1.0 / ENERGIES), totals[LAGS + lag] * (1.0 / ENERGIES)
        sums[0, lag * 8 : lag * 8 + 8] = p + pltpu.roll(p, BLOCK, 1)
        sums[1, lag * 8 : lag * 8 + 8] = q - pltpu.roll(q, BLOCK, 1)
    even, odd = pl.ds(0, 64, stride=2), pl.ds(1, 64, stride=2)
    out_ref[even, :] = jnp.where(lane, sums[0, even, :], sums[0, odd, :])
    out_ref[odd, :] = jnp.where(lane, -sums[1, even, :], sums[1, odd, :])

    rest = send.at[pl.ds(0, ENERGIES - 1)]
    pltpu.make_async_copy(rest, rest, send_sem).wait()


def per_device(retarded, lesser_sigma, coupling, coupling_pattern, kept_blocks, lead_lesser):
    hbm = pl.BlockSpec(memory_space=pl.ANY)
    smem = pl.BlockSpec(memory_space=pltpu.SMEM)
    f32, bf16 = jnp.float32, jnp.bfloat16
    out = pl.pallas_call(
        kernel,
        out_shape=jax.ShapeDtypeStruct((LAGS * 8, 128), f32),
        in_specs=[smem, smem, hbm, hbm, hbm, hbm],
        out_specs=pl.BlockSpec(memory_space=pltpu.VMEM),
        scratch_shapes=[
            pltpu.VMEM((2, 2, M, M), f32),
            pltpu.VMEM((2, 2, M, M), f32),
            pltpu.VMEM((2, 2, M, M), f32),
            pltpu.VMEM((2, M, M), f32),
            pltpu.VMEM((5, 3, M, M), bf16),
            pltpu.VMEM((5, 3, M, M), bf16),
            pltpu.VMEM((4, KEEP, 2 * BLOCK, 2 * M), bf16),
            pltpu.VMEM((2, 2, M, M), f32),
            pltpu.VMEM((2, M, M), f32),
            pltpu.VMEM((2, M, M), f32),
            pltpu.VMEM((ENERGIES, 8, 128), f32),
            pltpu.VMEM((ENERGIES + LAGS, 8, 128), f32),
            pltpu.VMEM((2, LAGS * 8, 128), f32),
            pltpu.SemaphoreType.DMA((7,)),
            pltpu.SemaphoreType.DMA((2,)),
            pltpu.SemaphoreType.DMA,
            pltpu.SemaphoreType.DMA,
        ],
        compiler_params=pltpu.CompilerParams(collective_id=0, has_side_effects=True),
        name="green_chain",
    )(coupling_pattern, kept_blocks, retarded, lesser_sigma, coupling, lead_lesser)
    tiles = out.reshape(LAGS, 4, 2, 128)
    return jnp.transpose(tiles, (0, 2, 1, 3)).reshape(LAGS, 2, 512)


def solution(mesh):
    return jax.shard_map(
        per_device,
        mesh=mesh,
        in_specs=(
            P("energy", "chain", None, None, None),
            P("energy", "chain", None, None, None),
            P("chain", None, None, None),
            P("chain", None, None),
            P(),
            P("energy", None, None, None),
        ),
        out_specs=P(None, None, ("chain", "energy")),
        check_vma=False,
    )
```

time: 112 us -> 24.2 us (0.22)
  the two profiles are of different devices: /device:TPU:0 before, /device:TPU:1 now
where the time goes in v1:
time: 24.2 us; the launch traced here: 24 us
  Pallas kernels  22.5 us (93%)
  local copies, waits for them, and re-layouts  1.47 us (6%)
    pallas_call x1, Pallas kernels, per_device(): pl.pallas_call(kernel, out_shape=jax.ShapeDtypeStruct((LAGS * 8, 128), f3...  22.5 us
    unnamed x1, local copies, waits for them, and re-layouts  1.47 us

profile of v1, /device:TPU:1, one launch (start us, length us, event | category | flops | bytes accessed | tf_op | source)
XLA Modules:
  0.0 24.0 jit_solution(13016724321034056043)
XLA Ops:
  0.0 22.5 %green_chain.1 = f32[128,128]{1,0:T(8,128)} custom-call(s32[2,4,4]{2,1,0:T(4,128)} %pattern_ref.1, s32[4]{0:T(128)} %kept_ref.1, f32[1,2,2,256,256]{4,3,2,1,0:T(8,128)} %g_hbm.1, f32[1,2,2,256,256]{4,3,2,1,0:T(8,128)} %s_hbm.1, f32[2,2,256,256]{3,2,1,0:T(8,128)} %b_hbm.1, f32[1,2,256,256]{3,2,1,0:T(8,128)} %lead_hbm.1), custom_call_target="tpu_custom_call" | custom-call | tf_op jit(solution)/shard_map/green_chain/pallas_call | solution.py:283
  22.5 1.5 %copy.9 = f32[16,2,512]{2,1,0:T(2,128)} copy(f32[16,2,512]{2,1,0:T(2,128)} %bitcast.5) | data formatting | bytes 131072

commit v2 on v1

--- a/solution.py
+++ b/solution.py
@@ -54,42 +54,22 @@
         return p - q, s - p - q
 
 
-def choose(which, blocks):
-    out = blocks[-1]
-    for i in range(len(blocks) - 2, -1, -1):
-        out = jnp.where(which == i, blocks[i], out)
-    return out
-
-
-def row_blocks(part):
-    return [part[i * BLOCK : (i + 1) * BLOCK] for i in range(NBLK)]
-
-
-def kept_left(rows_ref, re, im, kept_rows):
-    for k in range(KEEP):
-        for i, part in enumerate((re, im)):
-            high, low = split(choose(kept_rows[k], row_blocks(part)))
-            rows_ref[k, :BLOCK, i * M : (i + 1) * M] = high
-            rows_ref[k, BLOCK:, i * M : (i + 1) * M] = low
-
-
-def kept_tiles(rows_ref, re, im, kept_cols):
-    out = []
-    for k in range(KEEP):
-        re_h, re_l = split(choose(kept_cols[k], row_blocks(re)))
-        im_h, im_l = split(choose(kept_cols[k], row_blocks(im)))
-        stack = []
-        for x, y in ((re_h, im_h), (re_l, im_l)):
-            stack += [jnp.concatenate([x, y], 1), jnp.concatenate([-y, x], 1)]
-        o = lax.dot_general(rows_ref[k], jnp.concatenate(stack, 0), ADJ, preferred_element_type=jnp.float32)
-        o = o[:BLOCK] + o[BLOCK:]
-        out.append(o[:, :128] + o[:, 128:])
-    return out
+def planes(ref):
+    tiles = [ref[i] for i in range(16)]
+    rows = [jnp.concatenate(tiles[2 * i : 2 * i + 2], 1) for i in range(8)]
+    return jnp.concatenate(rows[:4], 0), jnp.concatenate(rows[4:], 0)
+
+
+def put_planes(ref, re, im):
+    for part, x in enumerate((re, im)):
+        for r in range(NBLK):
+            for t in range(2):
+                ref[part * 8 + r * 2 + t] = x[r * BLOCK : (r + 1) * BLOCK, t * 128 : (t + 1) * 128]
 
 
 def kernel(
     pattern_ref, kept_ref, g_hbm, s_hbm, b_hbm, lead_hbm, out_ref,
-    g_in, s_in, b_in, lead_in, left_h, left_l, rows, right, passed, entered, send, recv, sums,
+    g_in, s_in, b_in, lead_in, left_h, left_l, fresh_ref, grid0, grid1, entered, send, recv, sums,
     in_sem, pass_sem, send_sem, recv_sem,
 ):
     chain, me = lax.axis_index("chain"), lax.axis_index("energy")
@@ -109,11 +89,10 @@
 
     barrier = pltpu.get_barrier_semaphore()
 
-    @pl.loop(1, ENERGIES)
-    def _(step):
-        pl.semaphore_signal(
-            barrier, inc=1, device_id={"energy": lax.rem(me + step, ENERGIES)}, device_id_type=MESH
-        )
+    for step in range(1, ENERGIES):
+        other = me + step
+        other = jnp.where(other >= ENERGIES, other - ENERGIES, other)
+        pl.semaphore_signal(barrier, inc=1, device_id={"energy": other}, device_id_type=MESH)
 
     pl.semaphore_signal(barrier, inc=1, device_id={"chain": 1 - chain}, device_id_type=MESH)
 
@@ -135,18 +114,15 @@
             parts.append(jnp.concatenate(rows, 0))
         return parts
 
-    numbers = [jnp.full((BLOCK, M), kept_ref[k], jnp.int32) for k in range(KEEP)]
-    kept_rows = [jnp.right_shift(n, 2) for n in numbers]
-    kept_cols = [jnp.bitwise_and(n, 3) for n in numbers]
-
-    def keep_right(slot, re, im):
-        right[slot, 0], right[slot, 1] = re, im
-
-    def tiles_of(slot):
-        return kept_tiles(rows.at[slot], right[slot, 0], right[slot, 1], kept_cols)
-
-    def put(cell, tiles):
-        for k, tile in enumerate(tiles):
+    def put(cell, ref, re, im):
+        put_planes(ref, re, im)
+        for k in range(KEEP):
+            number = kept_ref[k]
+            at = jnp.right_shift(number, 1)
+            re_k, im_k = ref[at], ref[at + 8]
+            odd = jnp.full((BLOCK, 128), jnp.bitwise_and(number, 1), jnp.int32) == 1
+            still, moved = jnp.where(odd, im_k, re_k), pltpu.roll(jnp.where(odd, re_k, im_k), BLOCK, 1)
+            tile = jnp.where(lane != odd, still, moved)
             for row in range(8):
                 send[cell * 32 + k * 8 + row] = tile[row * 8 : row * 8 + 8]
 
@@ -170,9 +146,12 @@
                 ).start()
 
     passing = pltpu.make_async_remote_copy(
-        src_ref=passed, dst_ref=entered, send_sem=pass_sem.at[0], recv_sem=pass_sem.at[1],
+        src_ref=grid1, dst_ref=entered, send_sem=pass_sem.at[0], recv_sem=pass_sem.at[1],
         device_id={"chain": 1}, device_id_type=MESH,
     )
+
+    def plus(x, y):
+        return x[0] + y[0], x[1] + y[1]
 
     @pl.when(chain == 0)
     def _():
@@ -180,31 +159,25 @@
         b0, g0, b1, g1 = lefts[:4]
         b0.fill(*masked_coupling(0))
         loads["lead"].wait()
-        re, im = b0.adjoint(*b0.adjoint(lead_in[0], lead_in[1]))
+        inner = b0.adjoint(*b0.adjoint(lead_in[0], lead_in[1]))
         loads["s", 0].wait()
-        x_re, x_im = s_in[0, 0] + re, s_in[0, 1] + im
+        x = plus(inner, (s_in[0, 0], s_in[0, 1]))
         loads["g", 0].wait()
         g0.fill(g_in[0, 0], g_in[0, 1])
-        y_re, y_im = g0.adjoint(x_re, x_im)
-        keep_right(0, y_re, y_im)
-        state = g0.adjoint(y_re, y_im)
+        state = g0.adjoint(*g0.adjoint(*x))
+        put(0, grid0, *state)
         loads["b", 1].wait()
         b1.fill(*masked_coupling(1))
-        re, im = b1.adjoint(*b1.adjoint(*state))
+        inner = b1.adjoint(*b1.adjoint(*state))
         loads["s", 1].wait()
-        x_re, x_im = s_in[1, 0] + re, s_in[1, 1] + im
+        x = plus(inner, (s_in[1, 0], s_in[1, 1]))
         loads["g", 1].wait()
         g1.fill(g_in[1, 0], g_in[1, 1])
-        y_re, y_im = g1.adjoint(x_re, x_im)
-        keep_right(1, y_re, y_im)
-        passed[0], passed[1] = g1.adjoint(y_re, y_im)
+        state = g1.adjoint(*g1.adjoint(*x))
+        put(1, grid1, *state)
         pl.semaphore_wait(barrier, ENERGIES)
         passing.start()
-        kept_left(rows.at[0], g_in[0, 0], g_in[0, 1], kept_rows)
-        put(0, tiles_of(0))
         spread(0)
-        kept_left(rows.at[1], g_in[1, 0], g_in[1, 1], kept_rows)
-        put(1, tiles_of(1))
         spread(1)
         passing.wait_send()
 
@@ -214,39 +187,26 @@
         loads["s", 0].wait()
         loads["g", 0].wait()
         g2.fill(g_in[0, 0], g_in[0, 1])
-        y_re, y_im = g2.adjoint(s_in[0, 0], s_in[0, 1])
-        keep_right(0, y_re, y_im)
-        fresh = g2.adjoint(y_re, y_im)
-        kept_left(rows.at[0], g_in[0, 0], g_in[0, 1], kept_rows)
-        put(0, tiles_of(0))
+        fresh = g2.adjoint(*g2.adjoint(s_in[0, 0], s_in[0, 1]))
+        fresh_ref[0, 0], fresh_ref[0, 1] = fresh
         loads["b", 0].wait()
         joined = g2.plain(*masked_coupling(0))
         a2.fill(*joined)
         loads["b", 1].wait()
         b3.fill(*masked_coupling(1))
-        re, im = b3.adjoint(*b3.adjoint(*fresh))
+        inner = b3.adjoint(*b3.adjoint(*fresh))
         loads["s", 1].wait()
-        x_re, x_im = s_in[1, 0] + re, s_in[1, 1] + im
+        x = plus(inner, (s_in[1, 0], s_in[1, 1]))
         loads["g", 1].wait()
         g3.fill(g_in[1, 0], g_in[1, 1])
-        y_re, y_im = g3.adjoint(x_re, x_im)
-        keep_right(1, y_re, y_im)
-        kept_left(rows.at[1], g_in[1, 0], g_in[1, 1], kept_rows)
-        put(1, tiles_of(1))
-        c3_re, c3_im = g3.plain(*b3.plain(*joined))
-        c3.fill(c3_re, c3_im)
-        kept_left(rows.at[2], *joined, kept_rows)
-        kept_left(rows.at[3], c3_re, c3_im, kept_rows)
+        fresh_ref[1, 0], fresh_ref[1, 1] = g3.adjoint(*g3.adjoint(*x))
+        c3.fill(*g3.plain(*b3.plain(*joined)))
         loads["lead"].wait()
         pl.semaphore_wait(barrier, ENERGIES)
         passing.wait_recv()
-        for cell, left in ((0, a2), (1, c3)):
-            keep_right(cell, *left.adjoint(entered[0], entered[1]))
-            tiles = kept_tiles(rows.at[2 + cell], right[cell, 0], right[cell, 1], kept_cols)
-            for k in range(KEEP):
-                for row in range(8):
-                    at = cell * 32 + k * 8 + row
-                    send[at] = send[at] + tiles[k][row * 8 : row * 8 + 8]
+        for cell, left, ref in ((0, a2, grid0), (1, c3, grid1)):
+            change = left.adjoint(*left.adjoint(*planes(entered)))
+            put(cell, ref, *plus(change, (fresh_ref[cell, 0], fresh_ref[cell, 1])))
             spread(cell)
 
     everyone = recv.at[pl.ds(0, ENERGIES)]
@@ -265,7 +225,7 @@
 
     totals = lax.fori_loop(0, ENERGIES // 4, lag_step, (jnp.zeros((8, 128), jnp.float32),) * (2 * LAGS))
     for lag in range(LAGS):
-        p, q = totals[lag] * (1.0 / ENERGIES), totals[LAGS + lag] * (1.0 / ENERGIES)
+        p, q = totals[lag], totals[LAGS + lag]
         sums[0, lag * 8 : lag * 8 + 8] = p + pltpu.roll(p, BLOCK, 1)
         sums[1, lag * 8 : lag * 8 + 8] = q - pltpu.roll(q, BLOCK, 1)
     even, odd = pl.ds(0, 64, stride=2), pl.ds(1, 64, stride=2)
@@ -277,12 +237,12 @@
 
 
 def per_device(retarded, lesser_sigma, coupling, coupling_pattern, kept_blocks, lead_lesser):
-    hbm = pl.BlockSpec(memory_space=pl.ANY)
+    hbm = pl.BlockSpec(memory_space=pltpu.HBM)
     smem = pl.BlockSpec(memory_space=pltpu.SMEM)
     f32, bf16 = jnp.float32, jnp.bfloat16
     out = pl.pallas_call(
         kernel,
-        out_shape=jax.ShapeDtypeStruct((LAGS * 8, 128), f32),
+        out_shape=pltpu.VMEM((LAGS * 8, 128), f32),
         in_specs=[smem, smem, hbm, hbm, hbm, hbm],
         out_specs=pl.BlockSpec(memory_space=pltpu.VMEM),
         scratch_shapes=[
@@ -292,10 +252,10 @@
             pltpu.VMEM((2, M, M), f32),
             pltpu.VMEM((5, 3, M, M), bf16),
             pltpu.VMEM((5, 3, M, M), bf16),
-            pltpu.VMEM((4, KEEP, 2 * BLOCK, 2 * M), bf16),
-            pltpu.VMEM((2, 2, M, M), f32),
-            pltpu.VMEM((2, M, M), f32),
-            pltpu.VMEM((2, M, M), f32),
+            pltpu.VMEM((2, 2, M, M), f32),
+            pltpu.VMEM((16, BLOCK, 128), f32),
+            pltpu.VMEM((16, BLOCK, 128), f32),
+            pltpu.VMEM((16, BLOCK, 128), f32),
             pltpu.VMEM((ENERGIES, 8, 128), f32),
             pltpu.VMEM((ENERGIES + LAGS, 8, 128), f32),
             pltpu.VMEM((2, LAGS * 8, 128), f32),
@@ -308,7 +268,7 @@
         name="green_chain",
     )(coupling_pattern, kept_blocks, retarded, lesser_sigma, coupling, lead_lesser)
     tiles = out.reshape(LAGS, 4, 2, 128)
-    return jnp.transpose(tiles, (0, 2, 1, 3)).reshape(LAGS, 2, 512)
+    return jnp.transpose(tiles, (0, 2, 1, 3)).reshape(LAGS, 2, 512) * (1.0 / ENERGIES)
 
 
 def solution(mesh):

time: 24.2 us -> 22.5 us (0.930)
  local copies, waits for them, and re-layouts: 1.47 us -> 0 us
  Pallas kernels: 22.5 us -> 21.7 us
  other arithmetic: 0 us -> 0.64 us
    unnamed x1 -> x0, local copies, waits for them, and re-layouts: 1.47 us -> none
    pallas_call x1, Pallas kernels: 22.5 us -> 21.7 us  [per_device(): pl.pallas_call(kernel, out_shape=pltpu.VMEM((LAGS * 8, 128), f32), in_spe...]
    mul x0 -> x1, other arithmetic: none -> 0.64 us  [per_device(): jnp.transpose(tiles, (0, 2, 1, 3)).reshape(LAGS, 2, 512) * (1.0 / ENERGIES)]
where the time goes in v2:
time: 22.5 us; the launch traced here: 22.3 us
  Pallas kernels  21.7 us (96%)
  other arithmetic  0.64 us (3%)
    pallas_call x1, Pallas kernels, per_device(): pl.pallas_call(kernel, out_shape=pltpu.VMEM((LAGS * 8, 128), f32), in_spe...  21.7 us
    mul x1, other arithmetic, per_device(): jnp.transpose(tiles, (0, 2, 1, 3)).reshape(LAGS, 2, 512) * (1.0 / ENERGIES)  0.64 us

profile of v2, /device:TPU:1, one launch (start us, length us, event | category | flops | bytes accessed | tf_op | source)
XLA Modules:
  0.0 22.3 jit_solution(16247733762864801319)
XLA Ops:
  0.0 21.7 %green_chain.1 = f32[128,128]{1,0:T(8,128)S(1)} custom-call(s32[2,4,4]{2,1,0:T(4,128)} %pattern_ref.1, s32[4]{0:T(128)} %kept_ref.1, f32[1,2,2,256,256]{4,3,2,1,0:T(8,128)} %g_hbm.1, f32[1,2,2,256,256]{4,3,2,1,0:T(8,128)} %s_hbm.1, f32[2,2,256,256]{3,2,1,0:T(8,128)} %b_hbm.1, f32[1,2,256,256]{3,2,1,0:T(8,128)} %lead_hbm.1), custom_call_target="tpu_custom_call" | custom-call | tf_op jit(solution)/shard_map/green_chain/pallas_call | solution.py:243
  21.7 0.6 %broadcast_multiply_fusion = f32[128,128]{1,0:T(8,128)} fusion(f32[128,128]{1,0:T(8,128)S(1)} %green_chain.1), kind=kLoop, calls=%fused_computation | loop fusion | flops 16384 | bytes 131072 | tf_op jit(solution)/shard_map/mul | solution.py:271

commit v3 on v2

v3 whole, which is shorter than its diff:
```python
import functools

import jax
import jax.numpy as jnp
from jax import lax
from jax.experimental import pallas as pl
from jax.experimental.pallas import tpu as pltpu
from jax.sharding import PartitionSpec as P

M = 256
BLOCK = 64
NBLK = 4
KEEP = 4
LAGS = 16
ENERGIES = 64
SIDE = 4
MESH = pl.DeviceIdType.MESH
ADJ = (((1,), (1,)), ((), ()))
PLAIN = (((1,), (0,)), ((), ()))


def split(x):
    high = x.astype(jnp.bfloat16)
    return high, (x - high.astype(jnp.float32)).astype(jnp.bfloat16)


class Left:
    def __init__(self, high, low):
        self.high, self.low = high, low

    def fill(self, re, im):
        for i, part in enumerate((re, im, re + im)):
            self.high[i], self.low[i] = split(part)

    def times(self, parts, rows, dims):
        out = []
        for i, (right_h, right_l) in enumerate(parts):
            left_h, left_l = self.high[i, rows, :], self.low[i, rows, :]
            out.append(
                lax.dot_general(
                    jnp.concatenate([left_h, left_h, left_l], 1),
                    jnp.concatenate([right_h, right_l, right_h], 1 if dims is ADJ else 0),
                    dims,
                    preferred_element_type=jnp.float32,
                )
            )
        return out

    def adjoint(self, re, im, pieces=1):
        parts = [split(x) for x in (re, im, re - im)]
        size = M // pieces
        for piece in range(pieces):
            p, q, s = self.times(parts, slice(piece * size, (piece + 1) * size), ADJ)
            yield p + q, s - p + q

    def twice(self, re, im):
        (inner,) = self.adjoint(re, im)
        (outer,) = self.adjoint(*inner)
        return outer

    def plain(self, re, im):
        p, q, s = self.times([split(x) for x in (re, im, re + im)], slice(0, M), PLAIN)
        return p - q, s - p - q


def planes(ref):
    tiles = [ref[i] for i in range(16)]
    rows = [jnp.concatenate(tiles[2 * i : 2 * i + 2], 1) for i in range(8)]
    return jnp.concatenate(rows[:4], 0), jnp.concatenate(rows[4:], 0)


def put_planes(ref, re, im, first=0):
    for part, x in enumerate((re, im)):
        for r in range(x.shape[0] // BLOCK):
            for t in range(2):
                ref[part * 8 + (first + r) * 2 + t] = x[r * BLOCK : (r + 1) * BLOCK, t * 128 : (t + 1) * 128]


def kernel(
    pattern_hbm, kept_hbm, g_hbm, s_hbm, b_hbm, lead_hbm, out_ref,
    pattern_ref, kept_ref, g_in, s_in, b_in, lead_in, left_h, left_l, fresh_ref, joined, grid0, grid1, entered, extra, send, recv, sums,
    in_sem, pass_sem, back_sem, send_sem, recv_sem,
):
    chain, me = lax.axis_index("chain"), lax.axis_index("energy")
    my_y, my_x = lax.rem(lax.div(me, SIDE), SIDE), lax.rem(me, SIDE)

    def load(i, source, target):
        return pltpu.make_async_copy(source, target, in_sem.at[i])

    loads = {}
    for cell in range(2):
        loads["b", cell] = load(cell, b_hbm.at[cell], b_in.at[cell])
        loads["s", cell] = load(2 + cell, s_hbm.at[0, cell], s_in.at[cell])
        loads["g", cell] = load(4 + cell, g_hbm.at[0, cell], g_in.at[cell])
    loads["lead"] = load(6, lead_hbm.at[0], lead_in)
    loads["pattern"] = load(7, pattern_hbm, pattern_ref)
    loads["kept"] = load(8, kept_hbm, kept_ref)
    for name in ("pattern", ("b", 0), "lead", ("s", 0), ("g", 0), ("b", 1), ("s", 1), ("g", 1), "kept"):
        loads[name].start()

    barrier = pltpu.get_barrier_semaphore()

    for step in range(1, ENERGIES):
        other = me + step
        other = jnp.where(other >= ENERGIES, other - ENERGIES, other)
        pl.semaphore_signal(barrier, inc=1, device_id={"energy": other}, device_id_type=MESH)

    pl.semaphore_signal(barrier, inc=1, device_id={"chain": 1 - chain}, device_id_type=MESH)

    recv[pl.ds(ENERGIES, LAGS)] = jnp.zeros((LAGS, 8, 128), jnp.float32)
    lefts = [Left(left_h.at[i], left_l.at[i]) for i in range(5)]
    lane = lax.broadcasted_iota(jnp.int32, (BLOCK, 128), 1) < BLOCK

    def masked_coupling(cell):
        parts = []
        for part in range(2):
            rows = []
            for r in range(NBLK):
                strip = b_in[cell, part, r * BLOCK : (r + 1) * BLOCK, :]
                halves = []
                for t in range(NBLK // 2):
                    pair = [pattern_ref[cell, r, 2 * t + h].astype(jnp.float32) for h in range(2)]
                    halves.append(strip[:, t * 128 : (t + 1) * 128] * jnp.where(lane, pair[0], pair[1]))
                rows.append(jnp.concatenate(halves, 1))
            parts.append(jnp.concatenate(rows, 0))
        return parts

    def cut(ref):
        for k in range(KEEP):
            number = kept_ref[k]
            at = jnp.right_shift(number, 1)
            re_k, im_k = ref[at], ref[at + 8]
            odd = jnp.full((BLOCK, 128), jnp.bitwise_and(number, 1), jnp.int32) == 1
            still, moved = jnp.where(odd, im_k, re_k), pltpu.roll(jnp.where(odd, re_k, im_k), BLOCK, 1)
            tile = jnp.where(lane != odd, still, moved)
            for row in range(8):
                yield k * 8 + row, tile[row * 8 : row * 8 + 8]

    def turned(mine, by):
        at = mine + by
        return jnp.where(at >= SIDE, at - SIDE, at)

    offsets = (2, 3, 1, 0)
    across = {dx: turned(my_x, dx) for dx in offsets}
    lines = {dy: turned(my_y, dy) * SIDE for dy in offsets}

    def spread(cell):
        for dy in offsets:
            for dx in offsets:
                for z in (2 * cell, 2 * cell + 1):
                    owner = z * SIDE * SIDE + lines[dy] + across[dx]

                    def away(owner=owner):
                        pltpu.make_async_remote_copy(
                            src_ref=send.at[owner], dst_ref=recv.at[me], send_sem=send_sem, recv_sem=recv_sem,
                            device_id={"energy": owner}, device_id_type=MESH,
                        ).start()

                    def here(owner=owner):
                        pltpu.make_async_copy(send.at[owner], recv.at[me], recv_sem).start()

                    if dy or dx:
                        away()
                    else:
                        pl.when(owner != me)(away)
                        pl.when(owner == me)(here)

    def spread_next():
        for dy in offsets:
            for dx in offsets:
                for z in (0, 1):
                    owner = z * SIDE * SIDE + lines[dy] + across[dx]
                    pltpu.make_async_remote_copy(
                        src_ref=extra.at[owner], dst_ref=recv.at[me], send_sem=send_sem, recv_sem=recv_sem,
                        device_id={"chain": 1, "energy": owner}, device_id_type=MESH,
                    ).start()

    def partner_copy(source, target, sems, first, to):
        return pltpu.make_async_remote_copy(
            src_ref=source, dst_ref=target, send_sem=sems.at[first], recv_sem=sems.at[first + 1],
            device_id={"chain": to}, device_id_type=MESH,
        )

    passing = partner_copy(grid1, entered, pass_sem, 0, 1)
    back = partner_copy(joined, joined, back_sem, 0, 0)
    back_tiles = partner_copy(extra, extra, back_sem, 2, 0)

    def plus(x, y):
        return x[0] + y[0], x[1] + y[1]

    loads["pattern"].wait()

    @pl.when(chain == 0)
    def _():
        loads["b", 0].wait()
        b0, g0, b1, g1, a2 = lefts
        b0.fill(*masked_coupling(0))
        loads["lead"].wait()
        inner = b0.twice(lead_in[0], lead_in[1])
        loads["s", 0].wait()
        x = plus(inner, (s_in[0, 0], s_in[0, 1]))
        loads["g", 0].wait()
        g0.fill(g_in[0, 0], g_in[0, 1])
        state = g0.twice(*x)
        put_planes(grid0, *state)
        loads["kept"].wait()
        for at, tile in cut(grid0):
            send[at] = tile
        loads["b", 1].wait()
        b1.fill(*masked_coupling(1))
        inner = b1.twice(*state)
        loads["s", 1].wait()
        x = plus(inner, (s_in[1, 0], s_in[1, 1]))
        pl.semaphore_wait(barrier, ENERGIES)
        spread(0)
        loads["g", 1].wait()
        g1.fill(g_in[1, 0], g_in[1, 1])
        (y,) = g1.adjoint(*x)
        for half, (re, im) in enumerate(g1.adjoint(*y, pieces=2)):
            put_planes(grid1, re, im, first=2 * half)
            for part in range(2):
                piece = pl.ds(part * 8 + half * 4, 4)
                partner_copy(grid1.at[piece], entered.at[piece], pass_sem, 0, 1).start()
        back.wait_recv()
        a2.fill(joined[0], joined[1])
        put_planes(grid0, *a2.twice(*planes(grid1)))
        back_tiles.wait_recv()
        for at, tile in cut(grid0):
            extra[at] = extra[at] + tile
        spread_next()
        for at, tile in cut(grid1):
            send[32 + at] = tile
        spread(1)
        passing.wait_send()

    @pl.when(chain == 1)
    def _():
        g2, b3, g3, c3 = lefts[:4]
        loads["b", 0].wait()
        loads["g", 0].wait()
        g2.fill(g_in[0, 0], g_in[0, 1])
        joined[0], joined[1] = g2.plain(*masked_coupling(0))
        loads["s", 0].wait()
        fresh = g2.twice(s_in[0, 0], s_in[0, 1])
        put_planes(grid0, *fresh)
        loads["kept"].wait()
        for at, tile in cut(grid0):
            extra[at] = tile
        pl.semaphore_wait(barrier, ENERGIES)
        back.start()
        back_tiles.start()
        loads["b", 1].wait()
        b3.fill(*masked_coupling(1))
        inner = b3.twice(*fresh)
        loads["s", 1].wait()
        x = plus(inner, (s_in[1, 0], s_in[1, 1]))
        loads["g", 1].wait()
        g3.fill(g_in[1, 0], g_in[1, 1])
        fresh_ref[0], fresh_ref[1] = g3.twice(*x)
        c3.fill(*g3.plain(*b3.plain(joined[0], joined[1])))
        loads["lead"].wait()
        passing.wait_recv()
        put_planes(grid1, *plus(c3.twice(*planes(entered)), (fresh_ref[0], fresh_ref[1])))
        for at, tile in cut(grid1):
            send[32 + at] = tile
        spread(1)
        back.wait_send()
        back_tiles.wait_send()

    everyone = recv.at[pl.ds(0, ENERGIES)]
    pltpu.make_async_copy(everyone, everyone, recv_sem).wait()

    def lag_step(step, carry):
        first, second = list(carry[:LAGS]), list(carry[LAGS:])
        window = [recv[step * 4 + i] for i in range(LAGS + 3)]
        for i in range(4):
            earlier = window[i]
            swapped = pltpu.roll(earlier, BLOCK, 1)
            for lag in range(LAGS):
                first[lag] += window[i + lag] * earlier
                second[lag] += window[i + lag] * swapped
        return (*first, *second)

    totals = lax.fori_loop(0, ENERGIES // 4, lag_step, (jnp.zeros((8, 128), jnp.float32),) * (2 * LAGS))
    for lag in range(LAGS):
        p, q = totals[lag], totals[LAGS + lag]
        sums[0, lag * 8 : lag * 8 + 8] = p + pltpu.roll(p, BLOCK, 1)
        sums[1, lag * 8 : lag * 8 + 8] = q - pltpu.roll(q, BLOCK, 1)
    even, odd = pl.ds(0, 64, stride=2), pl.ds(1, 64, stride=2)
    out_ref[even, :] = jnp.where(lane, sums[0, even, :], sums[0, odd, :])
    out_ref[odd, :] = jnp.where(lane, -sums[1, even, :], sums[1, odd, :])

    def sent(tiles):
        some = recv.at[pl.ds(0, tiles)]
        pltpu.make_async_copy(some, some, send_sem).wait()

    @pl.when(chain == 0)
    def _():
        sent(63)
        sent(32)

    @pl.when(chain == 1)
    def _():
        sent(31)

        @pl.when(me < 32)
        def _():
            sent(1)


def per_device(retarded, lesser_sigma, coupling, coupling_pattern, kept_blocks, lead_lesser):
    hbm = pl.BlockSpec(memory_space=pltpu.HBM)
    f32, bf16 = jnp.float32, jnp.bfloat16
    out = pl.pallas_call(
        kernel,
        out_shape=pltpu.VMEM((LAGS * 8, 128), f32),
        in_specs=[hbm, hbm, hbm, hbm, hbm, hbm],
        out_specs=pl.BlockSpec(memory_space=pltpu.VMEM),
        scratch_shapes=[
            pltpu.SMEM((2, NBLK, NBLK), jnp.int32),
            pltpu.SMEM((KEEP,), jnp.int32),
            pltpu.VMEM((2, 2, M, M), f32),
            pltpu.VMEM((2, 2, M, M), f32),
            pltpu.VMEM((2, 2, M, M), f32),
            pltpu.VMEM((2, M, M), f32),
            pltpu.VMEM((5, 3, M, M), bf16),
            pltpu.VMEM((5, 3, M, M), bf16),
            pltpu.VMEM((2, M, M), f32),
            pltpu.VMEM((2, M, M), f32),
            pltpu.VMEM((16, BLOCK, 128), f32),
            pltpu.VMEM((16, BLOCK, 128), f32),
            pltpu.VMEM((16, BLOCK, 128), f32),
            pltpu.VMEM((32, 8, 128), f32),
            pltpu.VMEM((ENERGIES, 8, 128), f32),
            pltpu.VMEM((ENERGIES + LAGS, 8, 128), f32),
            pltpu.VMEM((2, LAGS * 8, 128), f32),
            pltpu.SemaphoreType.DMA((9,)),
            pltpu.SemaphoreType.DMA((2,)),
            pltpu.SemaphoreType.DMA((4,)),
            pltpu.SemaphoreType.DMA,
            pltpu.SemaphoreType.DMA,
        ],
        compiler_params=pltpu.CompilerParams(collective_id=0, has_side_effects=True),
        name="green_chain",
    )(coupling_pattern, kept_blocks, retarded, lesser_sigma, coupling, lead_lesser)
    tiles = out.reshape(LAGS, 4, 2, 128)
    return jnp.transpose(tiles, (0, 2, 1, 3)).reshape(LAGS, 2, 512) * (1.0 / ENERGIES)


def solution(mesh):
    return jax.shard_map(
        per_device,
        mesh=mesh,
        in_specs=(
            P("energy", "chain", None, None, None),
            P("energy", "chain", None, None, None),
            P("chain", None, None, None),
            P("chain", None, None),
            P(),
            P("energy", None, None, None),
        ),
        out_specs=P(None, None, ("chain", "energy")),
        check_vma=False,
    )
```

time: 22.5 us -> 21.4 us (0.951)
  Pallas kernels: 21.7 us -> 20.6 us
    pallas_call x1, Pallas kernels: 21.7 us -> 20.6 us  [per_device(): pl.pallas_call(kernel, out_shape=pltpu.VMEM((LAGS * 8, 128), f32), in_spe...]
where the time goes in v3:
time: 21.4 us; the launch traced here: 21.3 us
  Pallas kernels  20.6 us (96%)
  other arithmetic  0.64 us (3%)
    pallas_call x1, Pallas kernels, per_device(): pl.pallas_call(kernel, out_shape=pltpu.VMEM((LAGS * 8, 128), f32), in_spe...  20.6 us
    mul x1, other arithmetic, per_device(): jnp.transpose(tiles, (0, 2, 1, 3)).reshape(LAGS, 2, 512) * (1.0 / ENERGIES)  0.64 us

profile of v3, /device:TPU:1, one launch (start us, length us, event | category | flops | bytes accessed | tf_op | source)
XLA Modules:
  0.0 21.3 jit_solution(4893605159840891829)
XLA Ops:
  0.0 20.6 %green_chain.1 = f32[128,128]{1,0:T(8,128)S(1)} custom-call(s32[2,4,4]{2,1,0:T(4,128)} %pattern_hbm.1, s32[4]{0:T(128)} %kept_hbm.1, f32[1,2,2,256,256]{4,3,2,1,0:T(8,128)} %g_hbm.1, f32[1,2,2,256,256]{4,3,2,1,0:T(8,128)} %s_hbm.1, f32[2,2,256,256]{3,2,1,0:T(8,128)} %b_hbm.1, f32[1,2,256,256]{3,2,1,0:T(8,128)} %lead_hbm.1), custom_call_target="tpu_custom_call" | custom-call | tf_op jit(solution)/shard_map/green_chain/pallas_call | solution.py:314
  20.6 0.6 %broadcast_multiply_fusion = f32[128,128]{1,0:T(8,128)} fusion(f32[128,128]{1,0:T(8,128)S(1)} %green_chain.1), kind=kLoop, calls=%fused_computation | loop fusion | flops 16384 | bytes 131072 | tf_op jit(solution)/shard_map/mul | solution.py:347

commit v4 on v3

--- a/solution.py
+++ b/solution.py
@@ -14,6 +14,7 @@
 LAGS = 16
 ENERGIES = 64
 SIDE = 4
+LINES = ENERGIES // SIDE
 MESH = pl.DeviceIdType.MESH
 ADJ = (((1,), (1,)), ((), ()))
 PLAIN = (((1,), (0,)), ((), ()))
@@ -58,15 +59,12 @@
         (outer,) = self.adjoint(*inner)
         return outer
 
-    def plain(self, re, im):
-        p, q, s = self.times([split(x) for x in (re, im, re + im)], slice(0, M), PLAIN)
-        return p - q, s - p - q
-
-
-def planes(ref):
-    tiles = [ref[i] for i in range(16)]
-    rows = [jnp.concatenate(tiles[2 * i : 2 * i + 2], 1) for i in range(8)]
-    return jnp.concatenate(rows[:4], 0), jnp.concatenate(rows[4:], 0)
+    def plain(self, re, im, pieces=1):
+        parts = [split(x) for x in (re, im, re + im)]
+        size = M // pieces
+        for piece in range(pieces):
+            p, q, s = self.times(parts, slice(piece * size, (piece + 1) * size), PLAIN)
+            yield p - q, s - p - q
 
 
 def put_planes(ref, re, im, first=0):
@@ -78,8 +76,8 @@
 
 def kernel(
     pattern_hbm, kept_hbm, g_hbm, s_hbm, b_hbm, lead_hbm, out_ref,
-    pattern_ref, kept_ref, g_in, s_in, b_in, lead_in, left_h, left_l, fresh_ref, joined, grid0, grid1, entered, extra, send, recv, sums,
-    in_sem, pass_sem, back_sem, send_sem, recv_sem,
+    pattern_ref, kept_ref, g_in, s_in, b_in, lead_in, left_h, left_l, fresh_ref, joined, grid0, grid1, leaving, entered, g_far, extra, send, recv, seen, seen_swapped, sums,
+    in_sem, pass_sem, back_sem, send_sem, recv_sem, hello, go,
 ):
     chain, me = lax.axis_index("chain"), lax.axis_index("energy")
     my_y, my_x = lax.rem(lax.div(me, SIDE), SIDE), lax.rem(me, SIDE)
@@ -95,19 +93,37 @@
     loads["lead"] = load(6, lead_hbm.at[0], lead_in)
     loads["pattern"] = load(7, pattern_hbm, pattern_ref)
     loads["kept"] = load(8, kept_hbm, kept_ref)
-    for name in ("pattern", ("b", 0), "lead", ("s", 0), ("g", 0), ("b", 1), ("s", 1), ("g", 1), "kept"):
+    for name in ("pattern", ("b", 0), "lead", ("g", 0), ("s", 0), ("g", 1), ("b", 1), ("s", 1), "kept"):
         loads[name].start()
 
     barrier = pltpu.get_barrier_semaphore()
 
-    for step in range(1, ENERGIES):
-        other = me + step
-        other = jnp.where(other >= ENERGIES, other - ENERGIES, other)
-        pl.semaphore_signal(barrier, inc=1, device_id={"energy": other}, device_id_type=MESH)
-
-    pl.semaphore_signal(barrier, inc=1, device_id={"chain": 1 - chain}, device_id_type=MESH)
-
-    recv[pl.ds(ENERGIES, LAGS)] = jnp.zeros((LAGS, 8, 128), jnp.float32)
+    def turned(mine, by):
+        at = mine + by
+        return jnp.where(at >= SIDE, at - SIDE, at)
+
+    my_z = lax.div(me, SIDE * SIDE)
+    offsets = (2, 3, 1, 0)
+    across = {dx: turned(my_x, dx) for dx in offsets}
+    lines = {dy: turned(my_y, dy) * SIDE for dy in offsets}
+    planes_of = {dz: turned(my_z, dz) * SIDE * SIDE for dz in offsets}
+    steps = [(dz, dy, dx) for dz in offsets for dy in offsets for dx in offsets]
+    furthest_first = sorted(steps, key=lambda step: -sum(min(d, SIDE - d) for d in step))
+
+    @pl.when(chain == 1)
+    def _():
+        pl.semaphore_signal(barrier, inc=1, device_id={"chain": 0}, device_id_type=MESH)
+
+    for ref in (seen, seen_swapped):
+        ref[...] = jnp.zeros_like(ref)
+
+    def announce():
+        for dz, dy, dx in furthest_first[:-1]:
+            other = planes_of[dz] + lines[dy] + across[dx]
+            pl.semaphore_signal(barrier, inc=1, device_id={"chain": 1, "energy": other}, device_id_type=MESH)
+
+    my_line = lax.div(me, SIDE)
+    arrived = recv_sem.at[my_line]
     lefts = [Left(left_h.at[i], left_l.at[i]) for i in range(5)]
     lane = lax.broadcasted_iota(jnp.int32, (BLOCK, 128), 1) < BLOCK
 
@@ -136,14 +152,6 @@
             for row in range(8):
                 yield k * 8 + row, tile[row * 8 : row * 8 + 8]
 
-    def turned(mine, by):
-        at = mine + by
-        return jnp.where(at >= SIDE, at - SIDE, at)
-
-    offsets = (2, 3, 1, 0)
-    across = {dx: turned(my_x, dx) for dx in offsets}
-    lines = {dy: turned(my_y, dy) * SIDE for dy in offsets}
-
     def spread(cell):
         for dy in offsets:
             for dx in offsets:
@@ -152,12 +160,12 @@
 
                     def away(owner=owner):
                         pltpu.make_async_remote_copy(
-                            src_ref=send.at[owner], dst_ref=recv.at[me], send_sem=send_sem, recv_sem=recv_sem,
+                            src_ref=send.at[owner], dst_ref=recv.at[me], send_sem=send_sem, recv_sem=arrived,
                             device_id={"energy": owner}, device_id_type=MESH,
                         ).start()
 
                     def here(owner=owner):
-                        pltpu.make_async_copy(send.at[owner], recv.at[me], recv_sem).start()
+                        pltpu.make_async_copy(send.at[owner], recv.at[me], arrived).start()
 
                     if dy or dx:
                         away()
@@ -171,7 +179,7 @@
                 for z in (0, 1):
                     owner = z * SIDE * SIDE + lines[dy] + across[dx]
                     pltpu.make_async_remote_copy(
-                        src_ref=extra.at[owner], dst_ref=recv.at[me], send_sem=send_sem, recv_sem=recv_sem,
+                        src_ref=extra.at[owner], dst_ref=recv.at[me], send_sem=send_sem, recv_sem=arrived,
                         device_id={"chain": 1, "energy": owner}, device_id_type=MESH,
                     ).start()
 
@@ -181,107 +189,142 @@
             device_id={"chain": to}, device_id_type=MESH,
         )
 
-    passing = partner_copy(grid1, entered, pass_sem, 0, 1)
+
+    def plus(x, y):
+        return x[0] + y[0], x[1] + y[1]
+
+    loads["pattern"].wait()
+
+    passing = partner_copy(leaving, entered, pass_sem, 0, 1)
+    passing_g = partner_copy(g_hbm.at[0, 1], g_far, pass_sem, 2, 1)
     back = partner_copy(joined, joined, back_sem, 0, 0)
     back_tiles = partner_copy(extra, extra, back_sem, 2, 0)
 
-    def plus(x, y):
-        return x[0] + y[0], x[1] + y[1]
-
-    loads["pattern"].wait()
-
     @pl.when(chain == 0)
     def _():
-        loads["b", 0].wait()
-        b0, g0, b1, g1, a2 = lefts
+        pl.semaphore_signal(barrier, inc=1, device_id={"chain": 1}, device_id_type=MESH)
+        pl.semaphore_wait(barrier, 1)
+        passing_g.start()
+        pl.semaphore_signal(hello, inc=1, device_id={"chain": 1}, device_id_type=MESH)
+
+    announce()
+
+    def wait_for(*names):
+        for name in names:
+            loads[name].wait()
+
+    @pl.when(chain == 0)
+    def _():
+        b0, g0, b1, g1, d2 = lefts
+        wait_for(("b", 0))
         b0.fill(*masked_coupling(0))
-        loads["lead"].wait()
-        inner = b0.twice(lead_in[0], lead_in[1])
-        loads["s", 0].wait()
-        x = plus(inner, (s_in[0, 0], s_in[0, 1]))
-        loads["g", 0].wait()
+        wait_for("lead", ("s", 0), ("g", 0))
+        (inner,) = b0.adjoint(lead_in[0], lead_in[1])
         g0.fill(g_in[0, 0], g_in[0, 1])
-        state = g0.twice(*x)
+        (inner,) = b0.adjoint(*inner)
+        (y,) = g0.adjoint(*plus(inner, (s_in[0, 0], s_in[0, 1])))
+        wait_for(("b", 1), ("s", 1), ("g", 1), "kept")
+        b1.fill(*masked_coupling(1))
+        (state,) = g0.adjoint(*y)
         put_planes(grid0, *state)
-        loads["kept"].wait()
+        (inner,) = b1.adjoint(*state)
         for at, tile in cut(grid0):
             send[at] = tile
-        loads["b", 1].wait()
-        b1.fill(*masked_coupling(1))
-        inner = b1.twice(*state)
-        loads["s", 1].wait()
-        x = plus(inner, (s_in[1, 0], s_in[1, 1]))
-        pl.semaphore_wait(barrier, ENERGIES)
+        for half, pair in enumerate(b1.adjoint(*inner, pieces=2)):
+            some = pl.ds(half * (M // 2), M // 2)
+            for part in range(2):
+                leaving[part, some, :] = pair[part] + s_in[1, part, some, :]
+                partner_copy(leaving.at[part, some], entered.at[part, some], pass_sem, 0, 1).start()
+        back.wait_recv()
+        d2.fill(joined[0], joined[1])
+        put_planes(grid1, *d2.twice(leaving[0], leaving[1]))
+        back_tiles.wait_recv()
+        for at, tile in cut(grid1):
+            extra[at] = extra[at] + tile
+        pl.semaphore_wait(go, 1)
+        spread_next()
         spread(0)
-        loads["g", 1].wait()
         g1.fill(g_in[1, 0], g_in[1, 1])
-        (y,) = g1.adjoint(*x)
-        for half, (re, im) in enumerate(g1.adjoint(*y, pieces=2)):
-            put_planes(grid1, re, im, first=2 * half)
-            for part in range(2):
-                piece = pl.ds(part * 8 + half * 4, 4)
-                partner_copy(grid1.at[piece], entered.at[piece], pass_sem, 0, 1).start()
-        back.wait_recv()
-        a2.fill(joined[0], joined[1])
-        put_planes(grid0, *a2.twice(*planes(grid1)))
-        back_tiles.wait_recv()
+        put_planes(grid0, *g1.twice(leaving[0], leaving[1]))
         for at, tile in cut(grid0):
-            extra[at] = extra[at] + tile
-        spread_next()
-        for at, tile in cut(grid1):
             send[32 + at] = tile
         spread(1)
         passing.wait_send()
+        passing_g.wait_send()
 
     @pl.when(chain == 1)
     def _():
-        g2, b3, g3, c3 = lefts[:4]
-        loads["b", 0].wait()
-        loads["g", 0].wait()
+        g2, b3, g3, a2, d3 = lefts
+        wait_for(("g", 0))
         g2.fill(g_in[0, 0], g_in[0, 1])
-        joined[0], joined[1] = g2.plain(*masked_coupling(0))
-        loads["s", 0].wait()
+        wait_for(("b", 0), ("s", 0))
+        a2.fill(*next(g2.plain(*masked_coupling(0))))
         fresh = g2.twice(s_in[0, 0], s_in[0, 1])
+        wait_for(("b", 1), ("g", 1), ("s", 1), "kept", "lead")
+        passing_g.wait_recv()
+        pl.semaphore_wait(hello, 1)
+        for half, pair in enumerate(a2.plain(g_far[0], g_far[1], pieces=2)):
+            some = pl.ds(half * (M // 2), M // 2)
+            for part in range(2):
+                joined[part, some, :] = pair[part]
+                partner_copy(joined.at[part, some], joined.at[part, some], back_sem, 0, 0).start()
         put_planes(grid0, *fresh)
-        loads["kept"].wait()
         for at, tile in cut(grid0):
             extra[at] = tile
-        pl.semaphore_wait(barrier, ENERGIES)
-        back.start()
         back_tiles.start()
-        loads["b", 1].wait()
         b3.fill(*masked_coupling(1))
-        inner = b3.twice(*fresh)
-        loads["s", 1].wait()
-        x = plus(inner, (s_in[1, 0], s_in[1, 1]))
-        loads["g", 1].wait()
+        (inner,) = b3.adjoint(*fresh)
         g3.fill(g_in[1, 0], g_in[1, 1])
-        fresh_ref[0], fresh_ref[1] = g3.twice(*x)
-        c3.fill(*g3.plain(*b3.plain(joined[0], joined[1])))
-        loads["lead"].wait()
+        (inner,) = b3.adjoint(*inner)
+        (bridge,) = b3.plain(joined[0], joined[1])
+        (inner,) = g3.adjoint(*plus(inner, (s_in[1, 0], s_in[1, 1])))
+        pl.semaphore_wait(barrier, 2 * ENERGIES - 1)
+        pl.semaphore_signal(go, inc=1, device_id={"chain": 0}, device_id_type=MESH)
+        (state,) = g3.adjoint(*inner)
+        fresh_ref[0], fresh_ref[1] = state
+        d3.fill(*next(g3.plain(*bridge)))
         passing.wait_recv()
-        put_planes(grid1, *plus(c3.twice(*planes(entered)), (fresh_ref[0], fresh_ref[1])))
+        put_planes(grid1, *plus(d3.twice(entered[0], entered[1]), (fresh_ref[0], fresh_ref[1])))
         for at, tile in cut(grid1):
             send[32 + at] = tile
         spread(1)
         back.wait_send()
         back_tiles.wait_send()
 
-    everyone = recv.at[pl.ds(0, ENERGIES)]
-    pltpu.make_async_copy(everyone, everyone, recv_sem).wait()
-
-    def lag_step(step, carry):
+    order = (0, 1, 3, 2)
+
+    def line_step(step, carry):
         first, second = list(carry[:LAGS]), list(carry[LAGS:])
-        window = [recv[step * 4 + i] for i in range(LAGS + 3)]
-        for i in range(4):
-            earlier = window[i]
-            swapped = pltpu.roll(earlier, BLOCK, 1)
-            for lag in range(LAGS):
-                first[lag] += window[i + lag] * earlier
-                second[lag] += window[i + lag] * swapped
+        z = turned(my_z, order[step // SIDE])
+        y = turned(my_y, order[step % SIDE])
+        line = z * SIDE + y
+        mine = recv.at[pl.ds(line * SIDE, SIDE)]
+        pltpu.make_async_copy(mine, mine, recv_sem.at[line]).wait()
+        base = line * SIDE + LAGS
+        new = [recv[line * SIDE + i] for i in range(SIDE)]
+        swapped = [pltpu.roll(tile, BLOCK, 1) for tile in new]
+        for i in range(SIDE):
+            seen[base + i] = new[i]
+            seen_swapped[base + i] = swapped[i]
+        for ahead in range(LAGS + SIDE - 1):
+            later = new[ahead] if ahead < SIDE else seen[base + ahead]
+            for i in range(SIDE):
+                lag = ahead - i
+                if 0 <= lag < LAGS:
+                    first[lag] += later * new[i]
+                    second[lag] += later * swapped[i]
+        for behind in range(1, LAGS):
+            earlier, earlier_swapped = seen[base - behind], seen_swapped[base - behind]
+            for i in range(SIDE):
+                lag = behind + i
+                if lag < LAGS:
+                    first[lag] += new[i] * earlier
+                    second[lag] += new[i] * earlier_swapped
         return (*first, *second)
 
-    totals = lax.fori_loop(0, ENERGIES // 4, lag_step, (jnp.zeros((8, 128), jnp.float32),) * (2 * LAGS))
+    totals = (jnp.zeros((8, 128), jnp.float32),) * (2 * LAGS)
+    for step in range(LINES):
+        totals = line_step(step, totals)
     for lag in range(LAGS):
         p, q = totals[lag], totals[LAGS + lag]
         sums[0, lag * 8 : lag * 8 + 8] = p + pltpu.roll(p, BLOCK, 1)
@@ -329,16 +372,22 @@
             pltpu.VMEM((2, M, M), f32),
             pltpu.VMEM((16, BLOCK, 128), f32),
             pltpu.VMEM((16, BLOCK, 128), f32),
-            pltpu.VMEM((16, BLOCK, 128), f32),
+            pltpu.VMEM((2, M, M), f32),
+            pltpu.VMEM((2, M, M), f32),
+            pltpu.VMEM((2, M, M), f32),
             pltpu.VMEM((32, 8, 128), f32),
             pltpu.VMEM((ENERGIES, 8, 128), f32),
-            pltpu.VMEM((ENERGIES + LAGS, 8, 128), f32),
+            pltpu.VMEM((ENERGIES, 8, 128), f32),
+            pltpu.VMEM((ENERGIES + 2 * LAGS, 8, 128), f32),
+            pltpu.VMEM((ENERGIES + 2 * LAGS, 8, 128), f32),
             pltpu.VMEM((2, LAGS * 8, 128), f32),
             pltpu.SemaphoreType.DMA((9,)),
-            pltpu.SemaphoreType.DMA((2,)),
+            pltpu.SemaphoreType.DMA((4,)),
             pltpu.SemaphoreType.DMA((4,)),
             pltpu.SemaphoreType.DMA,
-            pltpu.SemaphoreType.DMA,
+            pltpu.SemaphoreType.DMA((LINES,)),
+            pltpu.SemaphoreType.REGULAR,
+            pltpu.SemaphoreType.REGULAR,
         ],
         compiler_params=pltpu.CompilerParams(collective_id=0, has_side_effects=True),
         name="green_chain",

time: 21.4 us -> 20 us (0.935)
  Pallas kernels: 20.6 us -> 19.1 us
    pallas_call x1, Pallas kernels: 20.6 us -> 19.1 us  [per_device(): pl.pallas_call(kernel, out_shape=pltpu.VMEM((LAGS * 8, 128), f32), in_spe...]
where the time goes in v4:
time: 20 us; the launch traced here: 19.7 us
  Pallas kernels  19.1 us (96%)
  other arithmetic  0.64 us (3%)
    pallas_call x1, Pallas kernels, per_device(): pl.pallas_call(kernel, out_shape=pltpu.VMEM((LAGS * 8, 128), f32), in_spe...  19.1 us
    mul x1, other arithmetic, per_device(): jnp.transpose(tiles, (0, 2, 1, 3)).reshape(LAGS, 2, 512) * (1.0 / ENERGIES)  0.64 us

profile of v4, /device:TPU:1, one launch (start us, length us, event | category | flops | bytes accessed | tf_op | source)
XLA Modules:
  0.0 19.7 jit_solution(17076171046333450866)
XLA Ops:
  0.0 19.1 %green_chain.1 = f32[128,128]{1,0:T(8,128)S(1)} custom-call(s32[2,4,4]{2,1,0:T(4,128)} %pattern_hbm.1, s32[4]{0:T(128)} %kept_hbm.1, f32[1,2,2,256,256]{4,3,2,1,0:T(8,128)} %g_hbm.1, f32[1,2,2,256,256]{4,3,2,1,0:T(8,128)} %s_hbm.1, f32[2,2,256,256]{3,2,1,0:T(8,128)} %b_hbm.1, f32[1,2,256,256]{3,2,1,0:T(8,128)} %lead_hbm.1), custom_call_target="tpu_custom_call" | custom-call | tf_op jit(solution)/shard_map/green_chain/pallas_call | solution.py:357
  19.1 0.6 %broadcast_multiply_fusion = f32[128,128]{1,0:T(8,128)} fusion(f32[128,128]{1,0:T(8,128)S(1)} %green_chain.1), kind=kLoop, calls=%fused_computation | loop fusion | flops 16384 | bytes 131072 | tf_op jit(solution)/shard_map/mul | solution.py:396

commit v5 on v4

--- a/solution.py
+++ b/solution.py
@@ -259,7 +259,7 @@
         g2.fill(g_in[0, 0], g_in[0, 1])
         wait_for(("b", 0), ("s", 0))
         a2.fill(*next(g2.plain(*masked_coupling(0))))
-        fresh = g2.twice(s_in[0, 0], s_in[0, 1])
+        (inner,) = g2.adjoint(s_in[0, 0], s_in[0, 1])
         wait_for(("b", 1), ("g", 1), ("s", 1), "kept", "lead")
         passing_g.wait_recv()
         pl.semaphore_wait(hello, 1)
@@ -268,6 +268,7 @@
             for part in range(2):
                 joined[part, some, :] = pair[part]
                 partner_copy(joined.at[part, some], joined.at[part, some], back_sem, 0, 0).start()
+        (fresh,) = g2.adjoint(*inner)
         put_planes(grid0, *fresh)
         for at, tile in cut(grid0):
             extra[at] = tile

time: 20 us -> 19.8 us (0.990)
  no operation moved by 1% of the time
where the time goes in v5:
time: 19.8 us; the launch traced here: 19.7 us
  Pallas kernels  19.1 us (96%)
  other arithmetic  0.64 us (3%)
    pallas_call x1, Pallas kernels, per_device(): pl.pallas_call(kernel, out_shape=pltpu.VMEM((LAGS * 8, 128), f32), in_spe...  19.1 us
    mul x1, other arithmetic, per_device(): jnp.transpose(tiles, (0, 2, 1, 3)).reshape(LAGS, 2, 512) * (1.0 / ENERGIES)  0.64 us

profile of v5, /device:TPU:1, one launch (start us, length us, event | category | flops | bytes accessed | tf_op | source)
XLA Modules:
  0.0 19.7 jit_solution(1739662643639487053)
XLA Ops:
  0.0 19.1 %green_chain.1 = f32[128,128]{1,0:T(8,128)S(1)} custom-call(s32[2,4,4]{2,1,0:T(4,128)} %pattern_hbm.1, s32[4]{0:T(128)} %kept_hbm.1, f32[1,2,2,256,256]{4,3,2,1,0:T(8,128)} %g_hbm.1, f32[1,2,2,256,256]{4,3,2,1,0:T(8,128)} %s_hbm.1, f32[2,2,256,256]{3,2,1,0:T(8,128)} %b_hbm.1, f32[1,2,256,256]{3,2,1,0:T(8,128)} %lead_hbm.1), custom_call_target="tpu_custom_call" | custom-call | tf_op jit(solution)/shard_map/green_chain/pallas_call | solution.py:358
  19.1 0.6 %broadcast_multiply_fusion = f32[128,128]{1,0:T(8,128)} fusion(f32[128,128]{1,0:T(8,128)S(1)} %green_chain.1), kind=kLoop, calls=%fused_computation | loop fusion | flops 16384 | bytes 131072 | tf_op jit(solution)/shard_map/mul | solution.py:397
